TPU v7x, 32 devices: a whole 2x2x4 slice. The times are simulated.
32 devices in a mesh: row: 2 (over x), col: 4 (over y, core), grid: 4 (over z).
Axes of the slice: x: 2, y: 2, z: 4, core: 2. Of those that a mesh axis runs over, the one named last changes fastest.
Arguments:
- snapshots: bfloat16 [16384, 1024], P(('row', 'col', 'grid')), may hold values from -6 to 6
- jitter_code: int32 [16384], replicated, may hold values from 0 to 63
- slab_start: int32 [4], P('grid'), may hold values from 0 to 127
- gamma: float32 [2048], P('grid'), may hold values from 0.1 to 10
- noise_var: float32 [1], replicated, may hold values from 0.3 to 1.5
Outputs:
- steered: float32 [16384, 2048], P(('row', 'col'), 'grid')
- gamma_new: float32 [2048], P('grid')
All inputs are finite; a program needn't handle non-finite values.
Results may differ from a plain program's by a relative error of at most 0.0003.
Values may be sent and summed in bfloat16 or wider, within the bound.
A program may use at most 64 MiB of HBM per device.

v0:
```python
import functools

import jax
import jax.numpy as jnp
from jax import lax
from jax.experimental import pallas as pl
from jax.experimental.pallas import tpu as pltpu
from jax.sharding import PartitionSpec as P

GRID = 65536
WIDTH = 256
F32 = jnp.float32
BF16 = jnp.bfloat16
MESH = pl.DeviceIdType.MESH


def sine(turns):
    z = turns * turns
    p = F32(39.53581371)
    p = p * z + F32(-76.54965682)
    p = p * z + F32(81.60099819)
    p = p * z + F32(-41.34165493)
    p = p * z + F32(6.28318516)
    return p * turns


def split(x):
    hi = x.astype(BF16)
    return hi, (x - hi.astype(F32)).astype(BF16)


def kernel(
    sizes, start_ref, pos_ref, snaps_ref, out_ref, forms_ref, norms_ref, last_ref, proj_hi, proj_lo,
    held, steer_hi, steer_lo, part, part_norm, full, *rest,
):
    n_row, n_col, n_grid, stride = sizes
    dims = [d for d in ((2, "core"), (n_col // 2, "y"), (n_row, "row")) if d[0] > 1]
    landed, sums = rest[: len(dims)], rest[len(dims) : 2 * len(dims)]
    load_sem, z_send, z_recv, p_send, p_recv = rest[2 * len(dims) :]
    n_block, _, rows, width = held.shape
    points = part.shape[1]
    snap = n_block * width
    row, col, z = (lax.axis_index(a) for a in ("row", "col", "grid"))
    place = {"core": col % 2, "y": col // 2, "row": row}

    def peer(kind, n, p):
        other = lax.rem(place[kind] + p, n)
        if kind == "row":
            return (other, col, z)
        if kind == "core":
            return (row, (col // 2) * 2 + other, z)
        return (row, other * 2 + col % 2, z)

    peers = [peer(kind, n, p) for n, kind in dims for p in range(1, n)]
    up, down = (row, col, z + 1), (row, col, z - 1)
    loads = [
        pltpu.make_async_copy(
            snaps_ref.at[:, pl.ds(k * width, width)], held.at[k, z], load_sem.at[k]
        )
        for k in range(n_block)
    ]
    for load in loads:
        load.start()
    barrier = pltpu.get_barrier_semaphore()
    for device in peers:
        pl.semaphore_signal(barrier, inc=1, device_id=device, device_id_type=MESH)

    @pl.when(z + 1 < n_grid)
    def _():
        pl.semaphore_signal(barrier, inc=1, device_id=up, device_id_type=MESH)

    @pl.when(z > 0)
    def _():
        pl.semaphore_signal(barrier, inc=1, device_id=down, device_id_type=MESH)

    beside = jnp.minimum(z, 1) + jnp.minimum(n_grid - 1 - z, 1)
    pl.semaphore_wait(barrier, len(peers) + beside)

    def hop(k, s, direction, origin):
        return pltpu.make_async_remote_copy(
            src_ref=held.at[k, origin],
            dst_ref=held.at[k, origin],
            send_sem=z_send.at[direction, k, s],
            recv_sem=z_recv.at[direction, k, s],
            device_id=up if direction == 0 else down,
            device_id_type=MESH,
        )

    def can_send(s, direction):
        if direction == 0:
            return jnp.logical_and(z + 1 < n_grid, z - s >= 0), z - s
        return jnp.logical_and(z > 0, z + s < n_grid), z + s

    def can_receive(s, direction):
        if direction == 0:
            return z - s - 1 >= 0, z - s - 1
        return z + s + 1 < n_grid, z + s + 1

    def send(k, s):
        for direction in (0, 1):
            ok, origin = can_send(s, direction)

            @pl.when(ok)
            def _():
                hop(k, s, direction, origin).start()

    def receive(k, s):
        for direction in (0, 1):
            ok, origin = can_receive(s, direction)

            @pl.when(ok)
            def _():
                hop(k, s, direction, origin).wait_recv()

    def drain(k, s):
        for direction in (0, 1):
            ok, origin = can_send(s, direction)

            @pl.when(ok)
            def _():
                hop(k, s, direction, origin).wait_send()

    def reduce_steps(source, target, turn):
        lanes = pl.ds(0, source.shape[1])
        offsets, sems, at, count = [], [], 0, 0
        length = points
        for n, kind in dims:
            length //= n
            offsets.append((at, length))
            at = at + place[kind] * length
            sems.append(count)
            count += n - 1

        def aligned(index):
            return pl.multiple_of(index, 8)

        def scatter(a):
            n, kind = dims[a]
            size = offsets[a][1]
            cur = source if a == 0 else sums[a - 1].at[:, lanes]
            copies = []
            yield
            for p in range(1, n):
                other = lax.rem(place[kind] + p, n)
                copy = pltpu.make_async_remote_copy(
                    src_ref=cur.at[pl.ds(aligned(other * size), size), :],
                    dst_ref=landed[a].at[turn, p - 1, :, lanes],
                    send_sem=p_send.at[2 * turn, sems[a] + p - 1],
                    recv_sem=p_recv.at[2 * turn, sems[a] + p - 1],
                    device_id=peer(kind, n, p),
                    device_id_type=MESH,
                )
                copy.start()
                copies.append(copy)
            yield
            for copy in copies:
                copy.wait()
            total = cur[pl.ds(aligned(place[kind] * size), size), :]
            for p in range(1, n):
                total = total + landed[a][turn, p - 1, :, lanes]
            if a + 1 < len(dims):
                sums[a][:, lanes] = total
            else:
                target[pl.ds(aligned(at), size), :] = total
            yield

        def gather(a):
            n, kind = dims[a]
            base, size = offsets[a]
            mine = pl.ds(aligned(base + place[kind] * size), size)
            copies = []
            yield
            for p in range(1, n):
                copy = pltpu.make_async_remote_copy(
                    src_ref=target.at[mine, :],
                    dst_ref=target.at[mine, :],
                    send_sem=p_send.at[2 * turn + 1, sems[a] + p - 1],
                    recv_sem=p_recv.at[2 * turn + 1, sems[a] + p - 1],
                    device_id=peer(kind, n, p),
                    device_id_type=MESH,
                )
                copy.start()
                copies.append(copy)
            yield
            for copy in copies:
                copy.wait()
            yield

        scatters = [scatter(a) for a in range(len(dims))]
        gathers = [gather(a) for a in reversed(range(len(dims)))]
        for step in scatters + gathers:
            next(step)
        return scatters, gathers

    def steer():
        part_norm[...] = jnp.zeros_like(part_norm)
        tile = 16
        tiles = points // tile

        def body(i, carry):
            g, first = i // tiles, pl.multiple_of((i % tiles) * tile, tile)
            pos = pos_ref[g]
            point = start_ref[0] + stride * (
                first + lax.broadcasted_iota(jnp.int32, (tile, 1), 0)
            )
            phase = (point * pos - ((pos & 127) << 15)) << 10
            turns = phase.astype(F32) * F32(2.0**-32)
            value = sine(0.25 - jnp.abs(turns))
            hi, lo = split(value)
            steer_hi[g, pl.ds(first, tile), :] = hi
            steer_lo[g, pl.ds(first, tile), :] = lo
            square = jnp.sum(value * value, axis=1, keepdims=True)
            part_norm[pl.ds(first, tile), :] += jnp.broadcast_to(square, (tile, 128))
            return carry

        lax.fori_loop(0, n_grid * tiles, body, 0)

    def project(k, origin, fresh=False):
        block = held[k, origin]
        value = jnp.dot(steer_hi[origin], block, preferred_element_type=F32)
        value += jnp.dot(steer_lo[origin], block, preferred_element_type=F32)
        if fresh:
            part[k % 2] = value
        else:
            part[k % 2] += value

    def project_arrived(k, s):
        for direction in (0, 1):
            ok, origin = can_receive(s, direction)

            @pl.when(ok)
            def _():
                project(k, origin)

    def prepare(k):
        value = full[k]
        square = jnp.sum(value * value, axis=1, keepdims=True)
        square = jnp.broadcast_to(square, (points, 128))
        forms_ref[...] = square if k == 0 else forms_ref[...] + square
        hi, lo = split(value / snap)
        proj_hi[...] = hi
        proj_lo[...] = lo

    def apply(k, first, count):
        dims_nt = (((1,), (1,)), ((), ()))

        def body(g, carry):
            block = held[k, g]
            added = lax.dot_general(block, proj_hi[...], dims_nt, preferred_element_type=F32)
            added += lax.dot_general(block, proj_lo[...], dims_nt, preferred_element_type=F32)
            spot = pl.ds(pl.multiple_of(g * rows, rows), rows)
            out_ref[spot, :] = added if k == 0 else out_ref[spot, :] + added
            return carry

        lax.fori_loop(first, first + count, body, 0)

    def applied(k, s, rounds):
        if k < 0:
            return
        if s == 0:
            prepare(k)
        first, end = n_grid * s // rounds, n_grid * (s + 1) // rounds
        if end > first:
            apply(k, first, end - first)

    loads[0].wait()
    send(0, 0)
    if n_block > 1:
        loads[1].wait()
        send(1, 0)
    for load in loads[2:]:
        load.wait()
    steer()
    rounds = n_grid - 1
    def advance(steps):
        for step in steps:
            next(step)

    def extra(*lists):
        for steps in lists:
            for step in steps[rounds:]:
                next(step)
                next(step)

    scatters, gathers = reduce_steps(part_norm, norms_ref, 1)
    waiting = []
    for k in range(n_block):
        for s in range(rounds):
            slot = scatters[s : s + 1] + waiting[s : s + 1]
            advance(slot)
            receive(k, s)
            if s + 1 < rounds:
                send(k, s + 1)
            if s + 2 == rounds and k + 2 < n_block:
                send(k + 2, 0)
            if s == 0:
                project(k, z, fresh=True)
            project_arrived(k, s)
            applied(k - 3, s, rounds)
            advance(slot)
        extra(scatters, waiting)
        waiting = gathers
        scatters, gathers = reduce_steps(part.at[k % 2], full.at[k], k % 2)
    last_ref[...] = held[n_block - 1]
    for steps, others, block in (
        (scatters, waiting, n_block - 3),
        (gathers, [], n_block - 2),
    ):
        for s in range(rounds):
            slot = steps[s : s + 1] + others[s : s + 1]
            advance(slot)
            applied(block, s, rounds)
            advance(slot)
        extra(steps, others)
    prepare(n_block - 1)
    for k in range(n_block):
        for s in range(n_grid - 1):
            drain(k, s)


def finish(partly_ref, held_ref, hi_ref, lo_ref, out_ref):
    dims_nt = (((1,), (1,)), ((), ()))
    block = held_ref[0]
    added = lax.dot_general(block, hi_ref[...], dims_nt, preferred_element_type=F32)
    added += lax.dot_general(block, lo_ref[...], dims_nt, preferred_element_type=F32)
    out_ref[...] = partly_ref[...] + added


def on_device(snapshots, jitter_code, slab_start, gamma, noise_var):
    n_row, n_col, n_grid = (lax.axis_size(a) for a in ("row", "col", "grid"))
    rows, snap = snapshots.shape
    group_rows = rows * n_grid
    points = gamma.shape[0]
    base = (lax.axis_index("row") * n_col + lax.axis_index("col")) * group_rows
    sensors = base + jnp.arange(group_rows, dtype=jnp.int32)
    pos = 64 * sensors + lax.dynamic_slice(jitter_code, (base,), (group_rows,)) + 32
    width = min(WIDTH, snap)
    n_block = snap // width
    dims = [n for n in (2, n_col // 2, n_row) if n > 1]
    landed, sums, length = [], [], points
    for n in dims:
        length //= n
        landed.append(pltpu.VMEM((2, n - 1, length, width), F32))
        sums.append(pltpu.VMEM((length, width), F32))
    n_peers = sum(n - 1 for n in dims)
    vmem = pl.BlockSpec(memory_space=pltpu.VMEM)
    partly, forms, norms, held, proj_hi, proj_lo = pl.pallas_call(
        functools.partial(kernel, (n_row, n_col, n_grid, GRID // points)),
        out_shape=(
            jax.ShapeDtypeStruct((group_rows, points), F32),
            jax.ShapeDtypeStruct((points, 128), F32),
            jax.ShapeDtypeStruct((points, 128), F32),
            jax.ShapeDtypeStruct((n_grid, rows, width), BF16),
            jax.ShapeDtypeStruct((points, width), BF16),
            jax.ShapeDtypeStruct((points, width), BF16),
        ),
        in_specs=[
            pl.BlockSpec(memory_space=pltpu.SMEM),
            vmem,
            pl.BlockSpec(memory_space=pl.ANY),
        ],
        out_specs=(vmem,) * 6,
        scratch_shapes=[
            pltpu.VMEM((n_block, n_grid, rows, width), BF16),
            pltpu.VMEM((n_grid, points, rows), BF16),
            pltpu.VMEM((n_grid, points, rows), BF16),
            pltpu.VMEM((2, points, width), F32),
            pltpu.VMEM((points, 128), F32),
            pltpu.VMEM((n_block, points, width), F32),
            *landed,
            *sums,
            pltpu.SemaphoreType.DMA((n_block,)),
            pltpu.SemaphoreType.DMA((2, n_block, n_grid - 1)),
            pltpu.SemaphoreType.DMA((2, n_block, n_grid - 1)),
            pltpu.SemaphoreType.DMA((4, n_peers)),
            pltpu.SemaphoreType.DMA((4, n_peers)),
        ],
        compiler_params=pltpu.CompilerParams(
            collective_id=0, has_side_effects=True, vmem_limit_bytes=56 << 20
        ),
    )(slab_start, pos.reshape(n_grid, 1, rows), snapshots)
    whole = pl.BlockSpec((points, width), lambda i: (0, 0))
    tile = pl.BlockSpec((rows, points), lambda i: (i, 0))
    steered = pl.pallas_call(
        finish,
        grid=(n_grid,),
        out_shape=jax.ShapeDtypeStruct((group_rows, points), F32),
        in_specs=[tile, pl.BlockSpec((1, rows, width), lambda i: (i, 0, 0)), whole, whole],
        out_specs=tile,
    )(partly, held, proj_hi, proj_lo)
    forms = forms[:, 0] / snap
    gamma_new = gamma * forms / (norms[:, 0] * (gamma + noise_var[0]))
    return (steered, gamma_new)


def solution(mesh):
    in_specs = (P(("row", "col", "grid"), None), P(), P("grid"), P("grid"), P())
    out_specs = (P(("row", "col"), "grid"), P("grid"))
    return jax.shard_map(
        on_device, mesh=mesh, in_specs=in_specs, out_specs=out_specs, check_vma=False
    )
```

profile of v0, /device:TPU:0, one launch (start us, length us, event | category | flops | bytes accessed | tf_op | source)
XLA Modules:
  0.0 117.4 jit_solution(16501196158931082336)
XLA Ops:
  0.6 1.3 %add_add_fusion = s32[2048]{0:T(1024)} fusion(s32[16384]{0:T(1024)} %param.6, s32[]{:T(128)S(6)} %select_n.3, s32[]{:T(128)S(6)} %mul.19), kind=kLoop, calls=%fused_computation.2 | loop fusion | flops 8192 | bytes 16392 | tf_op jit(solution)/shard_map/add | solution.py:336
  2.6 105.7 %shard_map.68 = (f32[2048,512]{1,0:T(8,128)}, f32[512,128]{1,0:T(8,128)}, f32[512,128]{1,0:T(8,128)}, bf16[4,512,256]{2,1,0:T(8,128)(2,1)}, bf16[512,256]{1,0:T(8,128)(2,1)}, /*index=5*/bf16[512,256]{1,0:T(8,128)(2,1)}) custom-call(s32[1]{0:T(128)S(6)} %copy.7.start_ref, s32[4,1,512]{2,1,0:T(1,128)} %bitcast.3, bf16[512,1024]{1,0:T(8,128)(2,1)} %snaps_ref.1), custom_call_target="tpu_custom_call" | custom-call | tf_op jit(solution)/shard_map/pallas_call | solution.py:347
  108.3 1.2 %slice_reduce_fusion = (f32[512]{0:T(512)S(1)}, f32[512]{0:T(512)S(1)}) fusion(f32[512,128]{1,0:T(8,128)} %get-tuple-element.13, f32[512,128]{1,0:T(8,128)} %get-tuple-element.12), kind=kLoop, calls=%fused_computation | loop fusion | flops 512 | bytes 8192 | tf_op jit(solution)/shard_map/slice | solution.py:392
  110.2 1.3 %multiply_divide_fusion = f32[512]{0:T(512)} fusion(f32[512]{0:T(512)S(1)} %get-tuple-element.14, f32[512]{0:T(512)} %param.8, f32[512]{0:T(512)S(1)} %get-tuple-element.15, f32[]{:T(128)} %bitcast.2), kind=kLoop, calls=%fused_computation.3 | loop fusion | flops 2048 | bytes 8196 | tf_op jit(solution)/shard_map/div | solution.py:392
  111.5 5.9 %shard_map.69 = f32[2048,512]{1,0:T(8,128)} custom-call(f32[2048,512]{1,0:T(8,128)} %get-tuple-element.8.partly_ref, bf16[4,512,256]{2,1,0:T(8,128)(2,1)} %get-tuple-element.9.held_ref, bf16[512,256]{1,0:T(8,128)(2,1)} %get-tuple-element.10.hi_ref, bf16[512,256]{1,0:T(8,128)(2,1)} %get-tuple-element.11.lo_ref), custom_call_target="tpu_custom_call" | custom-call | tf_op jit(solution)/shard_map/pallas_call | solution.py:384
where the time goes:
time: 118 us; the launch traced here: 117 us
  Pallas kernels  112 us (95%)
  other arithmetic  3.82 us (3%)
  between operations  1.96 us (2%)
    pallas_call x1, Pallas kernels, on_device(): pl.pallas_call(functools.partial(kernel, (n_row, n_col, n_grid, GRID // p...  106 us
    pallas_call x1, Pallas kernels, on_device(): pl.pallas_call(finish, grid=(n_grid,), out_shape=jax.ShapeDtypeStruct((gr...  5.87 us

commit v1 on v0

v1 whole, which is shorter than its diff:
```python
import functools

import jax
import jax.numpy as jnp
from jax import lax
from jax.experimental import pallas as pl
from jax.experimental.pallas import tpu as pltpu
from jax.sharding import PartitionSpec as P

GRID = 65536
WIDTH = 256
LANES = 128
F32 = jnp.float32
BF16 = jnp.bfloat16
MESH = pl.DeviceIdType.MESH


def sine(turns):
    z = turns * turns
    p = F32(39.53581371)
    p = p * z + F32(-76.54965682)
    p = p * z + F32(81.60099819)
    p = p * z + F32(-41.34165493)
    p = p * z + F32(6.28318516)
    return p * turns


def split(x):
    hi = x.astype(BF16)
    return hi, (x - hi.astype(F32)).astype(BF16)


def fold(x):
    n = x.shape[1]
    if n % LANES:
        total = jnp.sum(x, axis=1, keepdims=True)
        lane = lax.broadcasted_iota(jnp.int32, (x.shape[0], LANES), 1)
        return jnp.where(lane == 0, total, 0.0)
    return sum(x[:, a : a + LANES] for a in range(0, n, LANES))


def helped_blocks(n_grid, n_block):
    return list(range(n_block - n_block // 2, n_block)) if n_grid >= 4 else []


class Plan:
    def __init__(self, n_row, n_col, points):
        self.core = points // 2
        rest = [d for d in ((n_col // 2, "y"), (n_row, "row")) if d[0] > 1]
        total = 1
        for n, _ in rest:
            total *= n
        both = len(rest) == 2 and (self.core // total) % 16 == 0
        self.paths = [rest, rest[::-1]] if both else [rest]
        self.length = self.core // len(self.paths)
        self.shard = self.length // total
        self.depth = len(rest)
        at, event = 2 * self.core, 1
        self.land, self.sums, self.events, self.sizes = [], [], [], []
        for dims in self.paths:
            land, sums, events, sizes = [], [], [], []
            size = self.length
            for n, _ in dims:
                size //= n
                land.append(at)
                at += (n - 1) * size
                sums.append(at)
                at += size
                events.append(event)
                event += n - 1
                sizes.append(size)
            self.land.append(land)
            self.sums.append(sums)
            self.events.append(events)
            self.sizes.append(sizes)
        self.rows = at
        self.n_event = event


def kernel(
    sizes, start_ref, jitter_ref, snaps_ref, partly_ref, last_ref, hi_ref, lo_ref, forms_ref, norms_ref,
    held, steer_hi, steer_lo, far_hi, far_lo, parts, far_part, full, out, proj_hi, proj_lo, forms,
    part_norm, norms, work, work_norm, far_sum, far_in, jitter, positions, start_out, start_in,
    load_sem, misc_sem, z_send, z_recv, p_send, p_recv, f_send, f_recv, s_send, s_recv, o_sem,
):
    n_row, n_col, n_grid, stride = sizes
    n_block, _, rows, width = held.shape
    points = parts.shape[1]
    snap = n_block * width
    plan = Plan(n_row, n_col, points)
    helped = helped_blocks(n_grid, n_block)
    row, col, z = (lax.axis_index(a) for a in ("row", "col", "grid"))
    place = {"core": col % 2, "y": col // 2, "row": row}
    is_end = jnp.logical_or(z == 0, z == n_grid - 1)
    not_end = jnp.logical_not(is_end)
    helps = jnp.logical_or(z == 1, z == n_grid - 2)
    if not helped:
        is_end, not_end = None, None
    end_of = jnp.where(z == 1, 0, n_grid - 1)
    helper_of = jnp.where(z == 0, 1, n_grid - 2)

    def when(ok, action):
        if ok is None:
            action()
        else:
            pl.when(ok)(action)

    def peer(kind, other):
        if kind == "row":
            return (other, col, z)
        if kind == "core":
            return (row, (col // 2) * 2 + other, z)
        return (row, other * 2 + col % 2, z)

    def others(n, kind):
        return [lax.rem(place[kind] + p, n) for p in range(1, n)]

    peers = [peer("core", 1 - place["core"])]
    for n, kind in plan.paths[0]:
        peers += [peer(kind, other) for other in others(n, kind)]
    up, down = (row, col, z + 1), (row, col, z - 1)

    loads = [
        pltpu.make_async_copy(
            snaps_ref.at[:, pl.ds(k * width, width)], held.at[k, z], load_sem.at[k]
        )
        for k in range(n_block)
    ]
    for load in loads:
        load.start()
    codes = pltpu.make_async_copy(jitter_ref.at[row * n_col + col], jitter, misc_sem.at[0])
    codes.start()
    start_out[...] = jnp.full(start_out.shape, start_ref[0], jnp.int32)
    barrier = pltpu.get_barrier_semaphore()
    for device in peers:
        pl.semaphore_signal(barrier, inc=1, device_id=device, device_id_type=MESH)

    @pl.when(z + 1 < n_grid)
    def _():
        pl.semaphore_signal(barrier, inc=1, device_id=up, device_id_type=MESH)

    @pl.when(z > 0)
    def _():
        pl.semaphore_signal(barrier, inc=1, device_id=down, device_id_type=MESH)

    beside = jnp.minimum(z, 1) + jnp.minimum(n_grid - 1 - z, 1)
    pl.semaphore_wait(barrier, len(peers) + beside)


    def hop(k, s, direction, origin):
        return pltpu.make_async_remote_copy(
            src_ref=held.at[k, origin],
            dst_ref=held.at[k, origin],
            send_sem=z_send.at[direction, k, s],
            recv_sem=z_recv.at[direction, k, s],
            device_id=up if direction == 0 else down,
            device_id_type=MESH,
        )

    def can_send(s, direction):
        if direction == 0:
            return jnp.logical_and(z + 1 < n_grid, z - s >= 0), z - s
        return jnp.logical_and(z > 0, z + s < n_grid), z + s

    def can_receive(s, direction):
        if direction == 0:
            return z - s - 1 >= 0, z - s - 1
        return z + s + 1 < n_grid, z + s + 1

    def send(k, s, to_end=None):
        for direction in (0, 1):
            ok, origin = can_send(s, direction)
            if to_end is not None:
                last = z + 1 == n_grid - 1 if direction == 0 else z - 1 == 0
                ok = jnp.logical_and(ok, last if to_end else jnp.logical_not(last))

            @pl.when(ok)
            def _():
                hop(k, s, direction, origin).start()

    def receive(k, s, only=None):
        for direction in (0, 1):
            ok, origin = can_receive(s, direction)
            if only is not None:
                ok = jnp.logical_and(ok, only)

            @pl.when(ok)
            def _():
                hop(k, s, direction, origin).wait_recv()

    def drain(k, s):
        for direction in (0, 1):
            ok, origin = can_send(s, direction)

            @pl.when(ok)
            def _():
                hop(k, s, direction, origin).wait_send()

    def start_copy(device):
        return pltpu.make_async_remote_copy(
            src_ref=start_out,
            dst_ref=start_in,
            send_sem=s_send.at[0],
            recv_sem=s_recv.at[0],
            device_id=device,
            device_id_type=MESH,
        )

    if helped:
        pl.when(is_end)(lambda: start_copy((row, col, helper_of)).start())
    for k in range(n_block):
        loads[k].wait()
        send(k, 0)


    def aligned(index):
        return pl.multiple_of(index, 8)

    class Sum:
        def __init__(self, index, source, target, area, compact=False):
            self.index, self.source, self.target, self.area = index, source, target, area
            self.compact = compact

        def copy(self, src, dst, event, device):
            return pltpu.make_async_remote_copy(
                src_ref=src,
                dst_ref=dst,
                send_sem=p_send.at[self.index, event],
                recv_sem=p_recv.at[self.index, event],
                device_id=device,
                device_id_type=MESH,
            )

        def core_copy(self):
            other = 1 - place["core"]
            return self.copy(
                self.source.at[pl.ds(aligned(other * plan.core), plan.core), :],
                self.area.at[pl.ds(0, plan.core), :],
                0,
                peer("core", other),
            )

        def core_add(self):
            self.core_copy().wait()
            mine = pl.ds(aligned(place["core"] * plan.core), plan.core)
            self.area[pl.ds(plan.core, plan.core), :] = (
                self.source[mine, :] + self.area[pl.ds(0, plan.core), :]
            )

        def step_copies(self, j):
            copies = []
            for path, dims in enumerate(plan.paths):
                n, kind = dims[j]
                size = plan.sizes[path][j]
                base = plan.core + path * plan.length if j == 0 else plan.sums[path][j - 1]
                for p, other in enumerate(others(n, kind)):
                    copies.append(
                        self.copy(
                            self.area.at[pl.ds(aligned(base + other * size), size), :],
                            self.area.at[pl.ds(plan.land[path][j] + p * size, size), :],
                            plan.events[path][j] + p,
                            peer(kind, other),
                        )
                    )
            return copies

        def offset(self, path, j):
            at = place["core"] * plan.core + path * plan.length
            for (_, kind), size in zip(plan.paths[path][:j], plan.sizes[path][:j]):
                at = at + place[kind] * size
            return at

        def step_add(self, j):
            for copy in self.step_copies(j):
                copy.wait()
            for path, dims in enumerate(plan.paths):
                n, kind = dims[j]
                size = plan.sizes[path][j]
                base = plan.core + path * plan.length if j == 0 else plan.sums[path][j - 1]
                total = self.area[pl.ds(aligned(base + place[kind] * size), size), :]
                for p in range(n - 1):
                    total = total + self.area[pl.ds(plan.land[path][j] + p * size, size), :]
                if j + 1 < len(dims):
                    self.area[pl.ds(plan.sums[path][j], size), :] = total
                elif self.compact:
                    self.target[pl.ds(path * plan.shard, size), :] = total
                else:
                    self.target[pl.ds(aligned(self.offset(path, j + 1)), size), :] = total

        def step_back(self, j):
            copies = []
            for path, dims in enumerate(plan.paths):
                n, kind = dims[j]
                size = plan.sizes[path][j]
                mine = pl.ds(aligned(self.offset(path, j + 1)), size)
                for p, other in enumerate(others(n, kind)):
                    copies.append(
                        self.copy(
                            self.target.at[mine, :],
                            self.target.at[mine, :],
                            plan.n_event + plan.events[path][j] + p,
                            peer(kind, other),
                        )
                    )
            return copies

        def core_back(self):
            mine = pl.ds(aligned(place["core"] * plan.core), plan.core)
            return self.copy(
                self.target.at[mine, :],
                self.target.at[mine, :],
                plan.n_event,
                peer("core", 1 - place["core"]),
            )

        def scatter(self, ok=None):
            when(ok, lambda: self.core_copy().start())
            yield
            when(ok, self.core_add)
            for j in range(plan.depth):

                def go(j=j):
                    for copy in self.step_copies(j):
                        copy.start()

                when(ok, go)
                yield
                when(ok, functools.partial(self.step_add, j))

        def gather(self):
            for j in reversed(range(plan.depth)):
                for copy in self.step_back(j):
                    copy.start()
                yield
                for copy in self.step_back(j):
                    copy.wait()
            self.core_back().start()
            yield
            self.core_back().wait()

    active, summed, finished = [], [], []

    def tick(count=1):
        for _ in range(count):
            for steps in list(active):
                if next(steps, "end") == "end":
                    active.remove(steps)

    def spawn(steps):
        active.append(steps)
        next(steps)


    def find_positions():
        base = (row * n_col + col) * n_grid * rows
        for g in range(n_grid):
            sensor = base + g * rows + lax.broadcasted_iota(jnp.int32, (1, rows), 1)
            positions[g] = 64 * sensor + jitter[g] + 32

    def steer(first_point, count, group, hi_to, lo_to, norm):
        tile = min(32, points)
        tiles = points // tile

        def body(i, carry):
            j, first = i // tiles, pl.multiple_of((i % tiles) * tile, tile)
            pos = positions[group(j)]
            point = first_point() + stride * (
                first + lax.broadcasted_iota(jnp.int32, (tile, 1), 0)
            )
            phase = (point * pos - ((pos & 127) << 15)) << 10
            turns = phase.astype(F32) * F32(2.0**-32)
            value = sine(0.25 - jnp.abs(turns))
            hi, lo = split(value)
            hi_to[j, pl.ds(first, tile), :] = hi
            lo_to[j, pl.ds(first, tile), :] = lo
            if norm:
                part_norm[pl.ds(first, tile), :] += fold(value * value)
            return carry

        lax.fori_loop(0, count * tiles, body, 0)

    def far_group(j):
        return jnp.where(z == 1, z + 1 + j, j)

    def dots(hi, lo, block):
        value = jnp.dot(hi, block, preferred_element_type=F32)
        return value + jnp.dot(lo, block, preferred_element_type=F32)

    def project(k, origin, fresh=False):
        value = dots(steer_hi[origin], steer_lo[origin], held[k, origin])
        if fresh:
            parts[k] = value
        else:
            parts[k] += value

    def project_arrived(k, s, only=None):
        for direction in (0, 1):
            ok, origin = can_receive(s, direction)
            if only is not None:
                ok = jnp.logical_and(ok, only)

            @pl.when(ok)
            def _():
                project(k, origin)

    def project_far(k):
        i = helped.index(k)
        total = None
        for j in range(far_hi.shape[0]):
            value = dots(far_hi[j], far_lo[j], held[k, far_group(j)])
            total = value if total is None else total + value
        far_part[i] = total

    def far_copy(i):
        return pltpu.make_async_remote_copy(
            src_ref=far_sum.at[i],
            dst_ref=far_in.at[i],
            send_sem=f_send.at[i],
            recv_sem=f_recv.at[i],
            device_id=(row, col, end_of),
            device_id_type=MESH,
        )

    sums = [Sum(k, parts.at[k], full.at[k], work.at[k]) for k in range(n_block)]
    norm_sum = Sum(n_block, part_norm, norms, work_norm)
    far_sums = [
        Sum(n_block + 1 + i, far_part.at[i], far_sum.at[i], work.at[n_block + i], compact=True)
        for i in range(len(helped))
    ]

    def add_far(k):
        i = helped.index(k)
        far_copy(i).wait_recv()
        for path in range(len(plan.paths)):
            spot = pl.ds(aligned(sums[k].offset(path, plan.depth)), plan.shard)
            full[k, spot, :] += far_in[i, pl.ds(path * plan.shard, plan.shard), :]

    def reduce(k):
        yield from sums[k].scatter(not_end if k in helped else None)
        if k in helped:
            for other in range(helped[0]):
                if other in summed and other not in finished:
                    finish_block(other, is_end)
                    finished.append(other)
            when(is_end, functools.partial(add_far, k))
        yield from sums[k].gather()
        summed.append(k)

    def reduce_far(k):
        i = helped.index(k)
        yield from far_sums[i].scatter(helps)
        when(helps, lambda: far_copy(i).start())

    def reduce_norm():
        yield from norm_sum.scatter()
        yield from norm_sum.gather()

    def prepare(k):
        value = full[k]
        square = fold(value * value)
        forms[...] = square if k == 0 else forms[...] + square
        hi, lo = split(value / snap)
        proj_hi[k] = hi
        proj_lo[k] = lo

    def apply(k):
        dims_nt = (((1,), (1,)), ((), ()))

        def body(g, carry):
            block = held[k, g]
            added = lax.dot_general(block, proj_hi[k], dims_nt, preferred_element_type=F32)
            added += lax.dot_general(block, proj_lo[k], dims_nt, preferred_element_type=F32)
            spot = pl.ds(pl.multiple_of(g * rows, rows), rows)
            out[spot, :] = added if k == 0 else out[spot, :] + added
            return carry

        lax.fori_loop(0, n_grid, body, 0)

    def finish_block(k, only=None):
        def go():
            prepare(k)
            if k + 1 < n_block:
                apply(k)

        when(only, go)

    codes.wait()
    find_positions()
    part_norm[...] = jnp.zeros_like(part_norm)
    steer(lambda: start_ref[0], n_grid, lambda j: j, steer_hi, steer_lo, True)
    spawn(reduce_norm())
    for k in range(n_block):
        project(k, z, fresh=True)
    tick()
    if helped:

        @pl.when(helps)
        def _():
            start_copy((row, col, end_of)).wait_recv()
            steer(lambda: start_in[0:1, 0:1], n_grid - 2, far_group, far_hi, far_lo, False)

    tick()
    for k in range(n_block):
        receive(k, 0)
        if n_grid > 2:
            send(k, 1, to_end=False)
            if k not in helped:
                send(k, 1, to_end=True)
        project_arrived(k, 0)
        tick()
    early = [sums[k].scatter(is_end) for k in helped]
    for steps in early:
        next(steps)
    for _ in range(plan.depth + 1):
        for steps in early:
            next(steps, None)
    for k in range(n_block):
        if k in helped:
            continue
        for s in range(1, n_grid - 1):
            receive(k, s)
            if s + 1 < n_grid - 1:
                send(k, s + 1)
            project_arrived(k, s)
        spawn(reduce(k))
        tick(2)
    waiting = [(k, s) for k in helped for s in range(1, n_grid - 1)]
    for k in helped:
        for s in range(1, n_grid - 1):
            receive(k, s, not_end)
            if s + 1 < n_grid - 1:
                send(k, s + 1, to_end=False)
        send(*waiting.pop(0), to_end=True)
        for s in range(1, n_grid - 1):
            project_arrived(k, s, not_end)
        pl.when(helps)(functools.partial(project_far, k))
        spawn(reduce_far(k))
        spawn(reduce(k))
        tick(2)
    tick(2)
    for k, s in waiting:
        send(k, s, to_end=True)
    while active:
        tick()
    for k in range(n_block):
        if k in finished:
            finish_block(k, not_end)
            continue
        if k in helped and k + 1 < n_block:
            for s in range(1, n_grid - 1):
                receive(k, s, is_end)
        finish_block(k)

    outs = [
        pltpu.make_async_copy(src, dst, o_sem.at[i])
        for i, (src, dst) in enumerate(
            (
                (out, partly_ref),
                (proj_hi.at[n_block - 1], hi_ref),
                (proj_lo.at[n_block - 1], lo_ref),
                (forms, forms_ref),
                (norms, norms_ref),
                (held.at[n_block - 1], last_ref),
            )
        )
    ]
    for copy in outs[:-1]:
        copy.start()
    if helped:
        for s in range(1, n_grid - 1):
            receive(n_block - 1, s, is_end)
    outs[-1].start()
    for k in range(n_block):
        for s in range(n_grid - 1):
            drain(k, s)
    if helped:
        pl.when(is_end)(lambda: start_copy((row, col, helper_of)).wait_send())

        @pl.when(helps)
        def _():
            for i in range(len(helped)):
                far_copy(i).wait_send()

    for copy in outs:
        copy.wait()


def finish(snap, partly_ref, held_ref, hi_ref, lo_ref, forms_ref, norms_ref, gamma_ref, noise_ref, out_ref, new_ref):
    dims_nt = (((1,), (1,)), ((), ()))
    block = held_ref[...]
    added = lax.dot_general(block, hi_ref[...], dims_nt, preferred_element_type=F32)
    added += lax.dot_general(block, lo_ref[...], dims_nt, preferred_element_type=F32)
    out_ref[...] = partly_ref[...] + added

    @pl.when(pl.program_id(0) == 0)
    def _():
        form = jnp.sum(forms_ref[...].T, axis=0, keepdims=True) / snap
        norm = jnp.sum(norms_ref[...].T, axis=0, keepdims=True)
        gamma = gamma_ref[...]
        new_ref[...] = gamma * form / (norm * (gamma + noise_ref[0]))


def on_device(snapshots, jitter_code, slab_start, gamma, noise_var):
    n_row, n_col, n_grid = (lax.axis_size(a) for a in ("row", "col", "grid"))
    rows, snap = snapshots.shape
    group_rows = rows * n_grid
    points = gamma.shape[0]
    width = min(WIDTH, snap)
    n_block = snap // width
    plan = Plan(n_row, n_col, points)
    n_help = len(helped_blocks(n_grid, n_block))
    n_far = max(n_help, 1)
    shard = len(plan.paths) * plan.shard
    vmem = pl.BlockSpec(memory_space=pltpu.VMEM)
    any_space = pl.BlockSpec(memory_space=pl.ANY)
    n_sum = n_block + 1 + n_far
    dma = pltpu.SemaphoreType.DMA
    partly, last, hi, lo, forms, norms = pl.pallas_call(
        functools.partial(kernel, (n_row, n_col, n_grid, GRID // points)),
        out_shape=(
            jax.ShapeDtypeStruct((group_rows, points), F32),
            jax.ShapeDtypeStruct((n_grid, rows, width), BF16),
            jax.ShapeDtypeStruct((points, width), BF16),
            jax.ShapeDtypeStruct((points, width), BF16),
            jax.ShapeDtypeStruct((points, LANES), F32),
            jax.ShapeDtypeStruct((points, LANES), F32),
        ),
        in_specs=[pl.BlockSpec(memory_space=pltpu.SMEM), any_space, any_space],
        out_specs=(any_space,) * 6,
        scratch_shapes=[
            pltpu.VMEM((n_block, n_grid, rows, width), BF16),
            pltpu.VMEM((n_grid, points, rows), BF16),
            pltpu.VMEM((n_grid, points, rows), BF16),
            pltpu.VMEM((max(n_grid - 2, 1), points, rows), BF16),
            pltpu.VMEM((max(n_grid - 2, 1), points, rows), BF16),
            pltpu.VMEM((n_block, points, width), F32),
            pltpu.VMEM((n_far, points, width), F32),
            pltpu.VMEM((n_block, points, width), F32),
            pltpu.VMEM((group_rows, points), F32),
            pltpu.VMEM((n_block, points, width), BF16),
            pltpu.VMEM((n_block, points, width), BF16),
            pltpu.VMEM((points, LANES), F32),
            pltpu.VMEM((points, LANES), F32),
            pltpu.VMEM((points, LANES), F32),
            pltpu.VMEM((n_block + n_far, plan.rows, width), F32),
            pltpu.VMEM((plan.rows, LANES), F32),
            pltpu.VMEM((n_far, shard, width), F32),
            pltpu.VMEM((n_far, shard, width), F32),
            pltpu.VMEM((n_grid, 1, rows), jnp.int32),
            pltpu.VMEM((n_grid, 1, rows), jnp.int32),
            pltpu.VMEM((8, LANES), jnp.int32),
            pltpu.VMEM((8, LANES), jnp.int32),
            dma((n_block,)),
            dma((1,)),
            dma((2, n_block, n_grid - 1)),
            dma((2, n_block, n_grid - 1)),
            dma((n_sum, 2 * plan.n_event)),
            dma((n_sum, 2 * plan.n_event)),
            dma((n_far,)),
            dma((n_far,)),
            dma((1,)),
            dma((1,)),
            dma((6,)),
        ],
        compiler_params=pltpu.CompilerParams(
            collective_id=0, has_side_effects=True, vmem_limit_bytes=48 << 20
        ),
    )(slab_start, jitter_code.reshape(n_row * n_col, n_grid, 1, rows), snapshots)
    tile = min(256, group_rows)

    def whole(*shape):
        return pl.BlockSpec(shape, lambda i: (0, 0))

    def tall(columns):
        return pl.BlockSpec((tile, columns), lambda i: (i, 0))

    steered, gamma_new = pl.pallas_call(
        functools.partial(finish, snap),
        grid=(group_rows // tile,),
        out_shape=(
            jax.ShapeDtypeStruct((group_rows, points), F32),
            jax.ShapeDtypeStruct((1, points), F32),
        ),
        in_specs=[
            tall(points), tall(width), whole(points, width), whole(points, width),
            whole(points, LANES), whole(points, LANES), whole(1, points),
            pl.BlockSpec(memory_space=pltpu.SMEM),
        ],
        out_specs=(tall(points), whole(1, points)),
        compiler_params=pltpu.CompilerParams(vmem_limit_bytes=12 << 20),
    )(
        partly, last.reshape(group_rows, width), hi, lo, forms, norms,
        gamma.reshape(1, points), noise_var,
    )
    return (steered, gamma_new.reshape(points))


def solution(mesh):
    in_specs = (P(("row", "col", "grid"), None), P(), P("grid"), P("grid"), P())
    out_specs = (P(("row", "col"), "grid"), P("grid"))
    return jax.shard_map(
        on_device, mesh=mesh, in_specs=in_specs, out_specs=out_specs, check_vma=False
    )
```

time: 118 us -> 105 us (0.89)
  Pallas kernels: 112 us -> 97.5 us
  local copies, waits for them, and re-layouts: 0 us -> 4.92 us
  other arithmetic: 3.82 us -> 0 us
    pallas_call x1, Pallas kernels: 106 us -> 92.4 us  [on_device(): pl.pallas_call(functools.partial(kernel, (n_row, n_col, n_grid, GRID // p...]
    unnamed x0 -> x8, local copies, waits for them, and re-layouts: none -> 4.92 us
    add x1 -> x0, other arithmetic: 1.31 us -> none  [on_device(): 64 * sensors + lax.dynamic_slice(jitter_code, (base,), (group_rows,)) + 32]
    div x1 -> x0, other arithmetic: 1.27 us -> none  [on_device(): gamma_new = gamma * forms / (norms[:, 0] * (gamma + noise_var[0]))]
    slice x1 -> x0, other arithmetic: 1.24 us -> none  [on_device(): gamma_new = gamma * forms / (norms[:, 0] * (gamma + noise_var[0]))]
where the time goes in v1:
time: 105 us; the launch traced here: 104 us
  Pallas kernels  97.5 us (93%)
  local copies, waits for them, and re-layouts  4.92 us (5%)
  between operations  1.95 us (2%)
    pallas_call x1, Pallas kernels, on_device(): pl.pallas_call(functools.partial(kernel, (n_row, n_col, n_grid, GRID // p...  92.4 us
    pallas_call x1, Pallas kernels, on_device(): pl.pallas_call(functools.partial(finish, snap), grid=(group_rows // tile,...  5.06 us
    unnamed x8, local copies, waits for them, and re-layouts  4.92 us

profile of v1, /device:TPU:0, one launch (start us, length us, event | category | flops | bytes accessed | tf_op | source)
XLA Modules:
  0.0 104.3 jit_solution(15215391930780877967)
XLA Ops:
  1.9 0.0 copy-start.1
  1.9 1.2 %copy-done.1 = bf16[512,1024]{1,0:T(8,128)(2,1)S(1)} copy-done((bf16[512,1024]{1,0:T(8,128)(2,1)S(1)}, bf16[512,1024]{1,0:T(8,128)(2,1)}, u32[]{:S(2)}) %copy-start.1) | copy-done | bytes 1048600
  3.1 0.0 copy-start.2
  3.1 0.8 copy-done.2
  4.0 92.4 %shard_map.68 = (f32[2048,512]{1,0:T(8,128)}, bf16[4,512,256]{2,1,0:T(8,128)(2,1)S(1)}, bf16[512,256]{1,0:T(8,128)(2,1)S(1)}, bf16[512,256]{1,0:T(8,128)(2,1)S(1...) custom-call(s32[1]{0:T(128)S(6)} %copy.7.start_ref, s32[8,4,1,512]{3,2,1,0:T(1,128)S(1)} %bitcast.5, ...), custom_call_target="tpu_custom_call" | custom-call | tf_op jit(solution)/shard_map/pallas_call | solution.py:618
  96.4 0.0 copy-start
  96.4 2.2 %copy-done = f32[2048,512]{1,0:T(8,128)S(1)} copy-done((f32[2048,512]{1,0:T(8,128)S(1)}, f32[2048,512]{1,0:T(8,128)}, u32[]{:S(2)}) %copy-start) | copy-done | bytes 4194328
  98.6 0.0 copy-start.3
  98.6 0.7 copy-done.3
  99.3 5.1 %shard_map.69 = (f32[2048,512]{1,0:T(8,128)}, f32[1,512]{1,0:T(1,128)}) custom-call(f32[2048,512]{1,0:T(8,128)S(1)} %copy-done, bf16[2048,256]{1,0:T(8,128)(2,1)S(1)} %bitcast.4, bf16[512,256]{1,0:T(8,128)(2,1)S(1)} %get-tuple-element.12.hi_ref, bf16[512,256]{1,0:T(8,128)(2,1)S(1)} %get-tuple-element.13.lo_ref, f32[512,128]{1,0:T(8,128)S(1)} %get-tuple-element.14.forms_ref, ...), custom_call_target="tpu_custom_call" | custom-call | tf_op jit(solution)/shard_map/pallas_call | solution.py:677
Async XLA Ops:
  1.9 1.2 %copy-start.1 = (bf16[512,1024]{1,0:T(8,128)(2,1)S(1)}, bf16[512,1024]{1,0:T(8,128)(2,1)}, u32[]{:S(2)}) copy-start(bf16[512,1024]{1,0:T(8,128)(2,1)} %snaps_ref.1) | copy-start | bytes 3145732
  3.1 0.8 copy-start.2
  96.4 2.2 %copy-start = (f32[2048,512]{1,0:T(8,128)S(1)}, f32[2048,512]{1,0:T(8,128)}, u32[]{:S(2)}) copy-start(f32[2048,512]{1,0:T(8,128)} %get-tuple-element.10.partly_ref) | copy-start | bytes 12582916
  98.6 0.7 copy-start.3

commit v2 on v1

--- a/solution.py
+++ b/solution.py
@@ -327,16 +327,23 @@
                 yield
                 when(ok, functools.partial(self.step_add, j))
 
-        def gather(self):
+        def gather(self, ok=None):
             for j in reversed(range(plan.depth)):
-                for copy in self.step_back(j):
-                    copy.start()
+
+                def go(j=j):
+                    for copy in self.step_back(j):
+                        copy.start()
+
+                def land(j=j):
+                    for copy in self.step_back(j):
+                        copy.wait()
+
+                when(ok, go)
                 yield
-                for copy in self.step_back(j):
-                    copy.wait()
-            self.core_back().start()
+                when(ok, land)
+            when(ok, lambda: self.core_back().start())
             yield
-            self.core_back().wait()
+            when(ok, lambda: self.core_back().wait())
 
     active, summed, finished = [], [], []
 
@@ -437,14 +444,12 @@
 
     def reduce(k):
         yield from sums[k].scatter(not_end if k in helped else None)
-        if k in helped:
-            for other in range(helped[0]):
-                if other in summed and other not in finished:
-                    finish_block(other, is_end)
-                    finished.append(other)
-            when(is_end, functools.partial(add_far, k))
-        yield from sums[k].gather()
+        yield from sums[k].gather(not_end if k in helped else None)
         summed.append(k)
+
+    def gather_end(k):
+        when(is_end, functools.partial(add_far, k))
+        yield from sums[k].gather(is_end)
 
     def reduce_far(k):
         i = helped.index(k)
@@ -459,17 +464,15 @@
         value = full[k]
         square = fold(value * value)
         forms[...] = square if k == 0 else forms[...] + square
-        hi, lo = split(value / snap)
+        hi, lo = split((value / snap).T)
         proj_hi[k] = hi
         proj_lo[k] = lo
 
     def apply(k):
-        dims_nt = (((1,), (1,)), ((), ()))
-
         def body(g, carry):
             block = held[k, g]
-            added = lax.dot_general(block, proj_hi[k], dims_nt, preferred_element_type=F32)
-            added += lax.dot_general(block, proj_lo[k], dims_nt, preferred_element_type=F32)
+            added = jnp.dot(block, proj_hi[k], preferred_element_type=F32)
+            added += jnp.dot(block, proj_lo[k], preferred_element_type=F32)
             spot = pl.ds(pl.multiple_of(g * rows, rows), rows)
             out[spot, :] = added if k == 0 else out[spot, :] + added
             return carry
@@ -526,6 +529,7 @@
         tick(2)
     waiting = [(k, s) for k in helped for s in range(1, n_grid - 1)]
     for k in helped:
+        spawn(gather_end(k))
         for s in range(1, n_grid - 1):
             receive(k, s, not_end)
             if s + 1 < n_grid - 1:
@@ -586,10 +590,9 @@
 
 
 def finish(snap, partly_ref, held_ref, hi_ref, lo_ref, forms_ref, norms_ref, gamma_ref, noise_ref, out_ref, new_ref):
-    dims_nt = (((1,), (1,)), ((), ()))
     block = held_ref[...]
-    added = lax.dot_general(block, hi_ref[...], dims_nt, preferred_element_type=F32)
-    added += lax.dot_general(block, lo_ref[...], dims_nt, preferred_element_type=F32)
+    added = jnp.dot(block, hi_ref[...], preferred_element_type=F32)
+    added += jnp.dot(block, lo_ref[...], preferred_element_type=F32)
     out_ref[...] = partly_ref[...] + added
 
     @pl.when(pl.program_id(0) == 0)
@@ -620,8 +623,8 @@
         out_shape=(
             jax.ShapeDtypeStruct((group_rows, points), F32),
             jax.ShapeDtypeStruct((n_grid, rows, width), BF16),
-            jax.ShapeDtypeStruct((points, width), BF16),
-            jax.ShapeDtypeStruct((points, width), BF16),
+            jax.ShapeDtypeStruct((width, points), BF16),
+            jax.ShapeDtypeStruct((width, points), BF16),
             jax.ShapeDtypeStruct((points, LANES), F32),
             jax.ShapeDtypeStruct((points, LANES), F32),
         ),
@@ -637,8 +640,8 @@
             pltpu.VMEM((n_far, points, width), F32),
             pltpu.VMEM((n_block, points, width), F32),
             pltpu.VMEM((group_rows, points), F32),
-            pltpu.VMEM((n_block, points, width), BF16),
-            pltpu.VMEM((n_block, points, width), BF16),
+            pltpu.VMEM((n_block, width, points), BF16),
+            pltpu.VMEM((n_block, width, points), BF16),
             pltpu.VMEM((points, LANES), F32),
             pltpu.VMEM((points, LANES), F32),
             pltpu.VMEM((points, LANES), F32),
@@ -663,9 +666,15 @@
             dma((6,)),
         ],
         compiler_params=pltpu.CompilerParams(
-            collective_id=0, has_side_effects=True, vmem_limit_bytes=48 << 20
+            collective_id=0, has_side_effects=True, vmem_limit_bytes=34 << 20
         ),
-    )(slab_start, jitter_code.reshape(n_row * n_col, n_grid, 1, rows), snapshots)
+    )(
+        slab_start,
+        pltpu.with_memory_space_constraint(
+            jitter_code.reshape(n_row * n_col, n_grid, 1, rows), pltpu.MemorySpace.HBM
+        ),
+        pltpu.with_memory_space_constraint(snapshots, pltpu.MemorySpace.HBM),
+    )
     tile = min(256, group_rows)
 
     def whole(*shape):
@@ -682,7 +691,7 @@
             jax.ShapeDtypeStruct((1, points), F32),
         ),
         in_specs=[
-            tall(points), tall(width), whole(points, width), whole(points, width),
+            tall(points), tall(width), whole(width, points), whole(width, points),
             whole(points, LANES), whole(points, LANES), whole(1, points),
             pl.BlockSpec(memory_space=pltpu.SMEM),
         ],

time: 105 us -> 94.3 us (0.90)
  Pallas kernels: 97.5 us -> 91.5 us
  local copies, waits for them, and re-layouts: 4.92 us -> 0.68 us
    pallas_call x1, Pallas kernels: 92.4 us -> 86.6 us  [on_device(): pl.pallas_call(functools.partial(kernel, (n_row, n_col, n_grid, GRID // p...]
    unnamed x8 -> x2, local copies, waits for them, and re-layouts: 4.92 us -> 0.68 us
where the time goes in v2:
time: 94.3 us; the launch traced here: 94.1 us
  Pallas kernels  91.5 us (97%)
  between operations  1.94 us (2%)
    pallas_call x1, Pallas kernels, on_device(): pl.pallas_call(functools.partial(kernel, (n_row, n_col, n_grid, GRID // p...  86.6 us
    pallas_call x1, Pallas kernels, on_device(): pl.pallas_call(functools.partial(finish, snap), grid=(group_rows // tile,...  4.9 us

profile of v2, /device:TPU:0, one launch (start us, length us, event | category | flops | bytes accessed | tf_op | source)
XLA Modules:
  0.0 94.1 jit_solution(12645592606252802912)
XLA Ops:
  1.9 86.6 %shard_map.68 = (f32[2048,512]{1,0:T(8,128)S(1)}, bf16[4,512,256]{2,1,0:T(8,128)(2,1)S(1)}, bf16[256,512]{1,0:T(8,128)(2,1)S(1)}, bf16[256,512]{1,0:T(8,128)(2,1...) custom-call(s32[1]{0:T(128)S(6)} %copy.7.start_ref, s32[8,4,1,512]{3,2,1,0:T(1,128)} %bitcast.6, ...), custom_call_target="tpu_custom_call" | custom-call | tf_op jit(solution)/shard_map/pallas_call | solution.py:621
  88.5 0.0 copy-start
  88.5 0.7 copy-done
  89.2 4.9 %shard_map.69 = (f32[2048,512]{1,0:T(8,128)}, f32[1,512]{1,0:T(1,128)}) custom-call(f32[2048,512]{1,0:T(8,128)S(1)} %get-tuple-element.10.partly_ref, bf16[2048,256]{1,0:T(8,128)(2,1)S(1)} %bitcast.4, bf16[256,512]{1,0:T(8,128)(2,1)S(1)} %get-tuple-element.12.hi_ref, bf16[256,512]{1,0:T(8,128)(2,1)S(1)} %get-tuple-element.13.lo_ref, ...), custom_call_target="tpu_custom_call" | custom-call | tf_op jit(solution)/shard_map/pallas_call | solution.py:686
Async XLA Ops:
  88.5 0.7 copy-start

commit v3 on v2

--- a/solution.py
+++ b/solution.py
@@ -78,10 +78,10 @@
 
 
 def kernel(
-    sizes, start_ref, jitter_ref, snaps_ref, partly_ref, last_ref, hi_ref, lo_ref, forms_ref, norms_ref,
-    held, steer_hi, steer_lo, far_hi, far_lo, parts, far_part, full, out, proj_hi, proj_lo, forms,
+    sizes, start_ref, jitter_ref, snaps_ref, held_ref, hi_ref, lo_ref, forms_ref, norms_ref,
+    held, steer_hi, steer_lo, far_hi, far_lo, parts, far_part, full, proj_hi, proj_lo, forms,
     part_norm, norms, work, work_norm, far_sum, far_in, jitter, positions, start_out, start_in,
-    load_sem, misc_sem, z_send, z_recv, p_send, p_recv, f_send, f_recv, s_send, s_recv, o_sem,
+    load_sem, misc_sem, z_send, z_recv, p_send, p_recv, f_send, f_recv, s_send, s_recv, o_sem, h_sem,
 ):
     n_row, n_col, n_grid, stride = sizes
     n_block, _, rows, width = held.shape
@@ -178,6 +178,11 @@
             def _():
                 hop(k, s, direction, origin).start()
 
+    def keep(k, origin):
+        return pltpu.make_async_copy(
+            held.at[k, origin], held_ref.at[k, origin], h_sem.at[k, origin]
+        )
+
     def receive(k, s, only=None):
         for direction in (0, 1):
             ok, origin = can_receive(s, direction)
@@ -187,6 +192,7 @@
             @pl.when(ok)
             def _():
                 hop(k, s, direction, origin).wait_recv()
+                keep(k, origin).start()
 
     def drain(k, s):
         for direction in (0, 1):
@@ -211,6 +217,7 @@
     for k in range(n_block):
         loads[k].wait()
         send(k, 0)
+        keep(k, z).start()
 
 
     def aligned(index):
@@ -460,6 +467,12 @@
         yield from norm_sum.scatter()
         yield from norm_sum.gather()
 
+    def kept_projections(k):
+        return [
+            pltpu.make_async_copy(proj_hi.at[k], hi_ref.at[k], o_sem.at[2 * k]),
+            pltpu.make_async_copy(proj_lo.at[k], lo_ref.at[k], o_sem.at[2 * k + 1]),
+        ]
+
     def prepare(k):
         value = full[k]
         square = fold(value * value)
@@ -467,25 +480,8 @@
         hi, lo = split((value / snap).T)
         proj_hi[k] = hi
         proj_lo[k] = lo
-
-    def apply(k):
-        def body(g, carry):
-            block = held[k, g]
-            added = jnp.dot(block, proj_hi[k], preferred_element_type=F32)
-            added += jnp.dot(block, proj_lo[k], preferred_element_type=F32)
-            spot = pl.ds(pl.multiple_of(g * rows, rows), rows)
-            out[spot, :] = added if k == 0 else out[spot, :] + added
-            return carry
-
-        lax.fori_loop(0, n_grid, body, 0)
-
-    def finish_block(k, only=None):
-        def go():
-            prepare(k)
-            if k + 1 < n_block:
-                apply(k)
-
-        when(only, go)
+        for copy in kept_projections(k):
+            copy.start()
 
     codes.wait()
     find_positions()
@@ -544,36 +540,24 @@
     tick(2)
     for k, s in waiting:
         send(k, s, to_end=True)
+    for k in range(n_block):
+        if k in summed and k not in helped:
+            prepare(k)
+            finished.append(k)
     while active:
         tick()
     for k in range(n_block):
-        if k in finished:
-            finish_block(k, not_end)
-            continue
-        if k in helped and k + 1 < n_block:
-            for s in range(1, n_grid - 1):
-                receive(k, s, is_end)
-        finish_block(k)
-
+        if k not in finished:
+            prepare(k)
     outs = [
-        pltpu.make_async_copy(src, dst, o_sem.at[i])
-        for i, (src, dst) in enumerate(
-            (
-                (out, partly_ref),
-                (proj_hi.at[n_block - 1], hi_ref),
-                (proj_lo.at[n_block - 1], lo_ref),
-                (forms, forms_ref),
-                (norms, norms_ref),
-                (held.at[n_block - 1], last_ref),
-            )
-        )
+        pltpu.make_async_copy(src, dst, o_sem.at[2 * n_block + i])
+        for i, (src, dst) in enumerate(((forms, forms_ref), (norms, norms_ref)))
     ]
-    for copy in outs[:-1]:
+    for copy in outs:
         copy.start()
-    if helped:
+    for k in helped:
         for s in range(1, n_grid - 1):
-            receive(n_block - 1, s, is_end)
-    outs[-1].start()
+            receive(k, s, is_end)
     for k in range(n_block):
         for s in range(n_grid - 1):
             drain(k, s)
@@ -585,15 +569,20 @@
             for i in range(len(helped)):
                 far_copy(i).wait_send()
 
+    for k in range(n_block):
+        outs += kept_projections(k)
+        outs += [keep(k, g) for g in range(n_grid)]
     for copy in outs:
         copy.wait()
 
 
-def finish(snap, partly_ref, held_ref, hi_ref, lo_ref, forms_ref, norms_ref, gamma_ref, noise_ref, out_ref, new_ref):
-    block = held_ref[...]
-    added = jnp.dot(block, hi_ref[...], preferred_element_type=F32)
-    added += jnp.dot(block, lo_ref[...], preferred_element_type=F32)
-    out_ref[...] = partly_ref[...] + added
+def finish(snap, held_ref, hi_ref, lo_ref, forms_ref, norms_ref, gamma_ref, noise_ref, out_ref, new_ref):
+    total = None
+    for k in range(held_ref.shape[0]):
+        added = jnp.dot(held_ref[k], hi_ref[k], preferred_element_type=F32)
+        added += jnp.dot(held_ref[k], lo_ref[k], preferred_element_type=F32)
+        total = added if total is None else total + added
+    out_ref[...] = total
 
     @pl.when(pl.program_id(0) == 0)
     def _():
@@ -618,18 +607,17 @@
     any_space = pl.BlockSpec(memory_space=pl.ANY)
     n_sum = n_block + 1 + n_far
     dma = pltpu.SemaphoreType.DMA
-    partly, last, hi, lo, forms, norms = pl.pallas_call(
+    held, hi, lo, forms, norms = pl.pallas_call(
         functools.partial(kernel, (n_row, n_col, n_grid, GRID // points)),
         out_shape=(
-            jax.ShapeDtypeStruct((group_rows, points), F32),
-            jax.ShapeDtypeStruct((n_grid, rows, width), BF16),
-            jax.ShapeDtypeStruct((width, points), BF16),
-            jax.ShapeDtypeStruct((width, points), BF16),
+            jax.ShapeDtypeStruct((n_block, n_grid, rows, width), BF16),
+            jax.ShapeDtypeStruct((n_block, width, points), BF16),
+            jax.ShapeDtypeStruct((n_block, width, points), BF16),
             jax.ShapeDtypeStruct((points, LANES), F32),
             jax.ShapeDtypeStruct((points, LANES), F32),
         ),
         in_specs=[pl.BlockSpec(memory_space=pltpu.SMEM), any_space, any_space],
-        out_specs=(any_space,) * 6,
+        out_specs=(any_space,) * 5,
         scratch_shapes=[
             pltpu.VMEM((n_block, n_grid, rows, width), BF16),
             pltpu.VMEM((n_grid, points, rows), BF16),
@@ -639,7 +627,6 @@
             pltpu.VMEM((n_block, points, width), F32),
             pltpu.VMEM((n_far, points, width), F32),
             pltpu.VMEM((n_block, points, width), F32),
-            pltpu.VMEM((group_rows, points), F32),
             pltpu.VMEM((n_block, width, points), BF16),
             pltpu.VMEM((n_block, width, points), BF16),
             pltpu.VMEM((points, LANES), F32),
@@ -663,10 +650,11 @@
             dma((n_far,)),
             dma((1,)),
             dma((1,)),
-            dma((6,)),
+            dma((2 * n_block + 2,)),
+            dma((n_block, n_grid)),
         ],
         compiler_params=pltpu.CompilerParams(
-            collective_id=0, has_side_effects=True, vmem_limit_bytes=34 << 20
+            collective_id=0, has_side_effects=True, vmem_limit_bytes=32 << 20
         ),
     )(
         slab_start,
@@ -691,14 +679,16 @@
             jax.ShapeDtypeStruct((1, points), F32),
         ),
         in_specs=[
-            tall(points), tall(width), whole(width, points), whole(width, points),
+            pl.BlockSpec((n_block, tile, width), lambda i: (0, i, 0)),
+            pl.BlockSpec((n_block, width, points), lambda i: (0, 0, 0)),
+            pl.BlockSpec((n_block, width, points), lambda i: (0, 0, 0)),
             whole(points, LANES), whole(points, LANES), whole(1, points),
             pl.BlockSpec(memory_space=pltpu.SMEM),
         ],
         out_specs=(tall(points), whole(1, points)),
         compiler_params=pltpu.CompilerParams(vmem_limit_bytes=12 << 20),
     )(
-        partly, last.reshape(group_rows, width), hi, lo, forms, norms,
+        held.reshape(n_block, group_rows, width), hi, lo, forms, norms,
         gamma.reshape(1, points), noise_var,
     )
     return (steered, gamma_new.reshape(points))

time: 94.3 us -> 93.6 us (level)
    pallas_call x1, Pallas kernels: 86.6 us -> 83.7 us  [on_device(): pl.pallas_call(functools.partial(kernel, (n_row, n_col, n_grid, GRID // p...]
    pallas_call x1, Pallas kernels: 4.9 us -> 7.08 us  [on_device(): pl.pallas_call(functools.partial(finish, snap), grid=(group_rows // tile,...]
where the time goes in v3:
time: 93.6 us; the launch traced here: 93.4 us
  Pallas kernels  90.8 us (97%)
  between operations  1.94 us (2%)
    pallas_call x1, Pallas kernels, on_device(): pl.pallas_call(functools.partial(kernel, (n_row, n_col, n_grid, GRID // p...  83.7 us
    pallas_call x1, Pallas kernels, on_device(): pl.pallas_call(functools.partial(finish, snap), grid=(group_rows // tile,...  7.08 us

profile of v3, /device:TPU:0, one launch (start us, length us, event | category | flops | bytes accessed | tf_op | source)
XLA Modules:
  0.0 93.4 jit_solution(1811263199475698477)
XLA Ops:
  1.9 83.7 %shard_map.68 = (bf16[4,4,512,256]{3,2,1,0:T(8,128)(2,1)S(1)}, bf16[4,256,512]{2,1,0:T(8,128)(2,1)S(1)}, bf16[4,256,512]{2,1,0:T(8,128)(2,1)S(1)}, f32[512,128]{1,0:T(8,128)S(1)}, f32[512,128]{1,0:T(8,128)S(1)}) custom-call(s32[1]{0:T(128)S(6)} %copy.7.start_ref, s32[8,4,1,512]{3,2,1,0:T(1,128)} %bitcast.6, bf16[512,1024]{1,0:T(8,128)(2,1)} %snaps_ref.1), custom_call_target="tpu_custom_call" | custom-call | tf_op jit(solution)/shard_map/pallas_call | solution.py:610
  85.6 0.0 copy-start
  85.6 0.7 copy-done
  86.3 7.1 %shard_map.69 = (f32[2048,512]{1,0:T(8,128)}, f32[1,512]{1,0:T(1,128)}) custom-call(bf16[4,2048,256]{2,1,0:T(8,128)(2,1)S(1)} %bitcast.4, bf16[4,256,512]{2,1,0:T(8,128)(2,1)S(1)} %get-tuple-element.10.hi_ref, bf16[4,256,512]{2,1,0:T(8,128)(2,1)S(1)} %get-tuple-element.11.lo_ref, f32[512,128]{1,0:T(8,128)S(1)} %get-tuple-element.12.forms_ref, ...), custom_call_target="tpu_custom_call" | custom-call | tf_op jit(solution)/shard_map/pallas_call | solution.py:674
Async XLA Ops:
  85.6 0.7 copy-start
